TPU v7x, 512 devices: a whole 4x8x8 slice. The times are simulated.
512 devices in a mesh: chan: 8 (over z), sx: 8 (over x, core), sy: 8 (over y).
Axes of the slice: x: 4, y: 8, z: 8, core: 2. Of those that a mesh axis runs over, the one named last changes fastest.
Arguments:
- volume: bfloat16 [8, 64, 64, 256], P('sx', 'sy', None, 'chan'), may hold values from -6 to 6
- kernel: bfloat16 [27, 256, 256], P(None, 'chan'), may hold values from -0.078125 to 0.078125
- grad_out: bfloat16 [8, 64, 64, 256], P('sx', 'sy', None, 'chan'), may hold values from -6 to 6
Outputs:
- out: bfloat16 [8, 64, 64, 256], P('sx', 'sy', None, 'chan')
- grad_input: bfloat16 [8, 64, 64, 256], P('sx', 'sy', None, 'chan')
- grad_kernel: float32 [27, 256, 256], P(None, 'chan')
All inputs are finite; a program needn't handle non-finite values.
Results may differ from a plain program's by a relative error of at most 0.0015.
Values may be sent and summed in bfloat16 or wider, within the bound.
No kernel may reach another device: no remote copies, remote signals or barrier semaphores. Data moves between devices by JAX's collectives and lax.ppermute only.
A program may use at most 64 MiB of HBM per device.

v0:
```python
import math
import jax
import jax.numpy as jnp
from jax import lax
from jax.sharding import PartitionSpec as P


def padded_2(shard, sides, width):
    for axis, dim in sides:
        count, length = (lax.axis_size(axis), shard.shape[dim])
        up = [(i, (i + 1) % count) for i in range(count - 1)]
        down = [(j, i) for i, j in up]
        last = lax.slice_in_dim(shard, length - width, length, axis=dim)
        leading = lax.slice_in_dim(shard, 0, width, axis=dim)
        before = lax.ppermute(last, axis, up)
        after = lax.ppermute(leading, axis, down)
        shard = jnp.concatenate([before, shard, after], axis=dim)
    return shard


def body(volume, kernel, grad_out):
    size_x, size_y, size_z, own_in = volume.shape
    total_out = kernel.shape[2]
    cells = size_x * size_y * size_z
    rim = padded_2(volume, (("sx", 0), ("sy", 1)), 1)
    padded = jnp.pad(rim, ((0, 0), (0, 0), (1, 1), (0, 0)))
    offsets = [(index // 9, index // 3 % 3, index % 3) for index in range(27)]
    partial_out = jnp.zeros((cells, total_out), jnp.float32)
    for index in range(27):
        a, b, e = offsets[index]
        window = padded[a : a + size_x, b : b + size_y, e : e + size_z].reshape(cells, own_in)
        partial_out = partial_out + jnp.dot(
            window, kernel[index], preferred_element_type=jnp.float32
        )
    partial_out = partial_out.reshape(size_x, size_y, size_z, total_out)
    out = lax.psum_scatter(partial_out, "chan", scatter_dimension=3, tiled=True).astype(
        jnp.bfloat16
    )
    grad_full = lax.all_gather(grad_out, "chan", axis=3, tiled=True)
    grad_rimmed = padded_2(grad_full, (("sx", 0), ("sy", 1)), 1)
    grad_padded = jnp.pad(grad_rimmed, ((0, 0), (0, 0), (1, 1), (0, 0)))
    flat_grad = grad_full.reshape(cells, total_out)
    back = jnp.zeros((cells, own_in), jnp.float32)
    kernel_terms = []
    for index in range(27):
        a, b, e = offsets[index]
        window = grad_padded[
            2 - a : 2 - a + size_x, 2 - b : 2 - b + size_y, 2 - e : 2 - e + size_z
        ].reshape(cells, total_out)
        back = back + lax.dot_general(
            window, kernel[index], (((1,), (1,)), ((), ())), preferred_element_type=jnp.float32
        )
        in_window = padded[a : a + size_x, b : b + size_y, e : e + size_z].reshape(cells, own_in)
        kernel_terms.append(
            lax.dot_general(
                in_window, flat_grad, (((0,), (0,)), ((), ())), preferred_element_type=jnp.float32
            )
        )
    grad_input = back.reshape(size_x, size_y, size_z, own_in).astype(jnp.bfloat16)
    local_kernel = jnp.stack(kernel_terms)
    summed = lax.psum(local_kernel, ("sx", "sy"))
    all_cells = cells * lax.axis_size("sx") * lax.axis_size("sy")
    grad_kernel = summed / jnp.float32(math.sqrt(all_cells))
    return (out, grad_input, grad_kernel)


def solution(mesh):
    return jax.shard_map(
        body,
        mesh=mesh,
        in_specs=(P("sx", "sy", None, "chan"), P(None, "chan", None), P("sx", "sy", None, "chan")),
        out_specs=(P("sx", "sy", None, "chan"), P("sx", "sy", None, "chan"), P(None, "chan", None)),
        check_vma=False,
    )
```

profile of v0, /device:TPU:25, one launch (start us, length us, event | category | flops | bytes accessed | tf_op | source)
XLA Modules:
  0.0 342.9 jit_solution(3898932481704692713)
XLA Ops:
  8.1 3.7 %collective-permute-start = (bf16[1,8,64,32]{2,3,1,0:T(8,128)(2,1)}, bf16[1,8,64,32]{2,3,1,0:T(8,128)(2,1)S(1)}, u32[]{:S(2)}, u32[]{:S(2)}) collective-permute-start(bf16[1,8,64,32]{2,3,1,0:T(8,128)(2,1)} %param.3), channel_id=1, source_target_pairs={{0,8},{8,16},{16,24},{24,32},{32,40},{40,48},{48,56},{1,9},{9,17},... | collective-permute-start | bytes 98312 | tf_op jit(solution)/shard_map/ppermute | solution.py:15
  11.7 1.9 collective-permute-start.1
  15.5 2.1 collective-permute-done.1
  17.6 2.1 collective-permute-start.3
  19.7 4.4 %collective-permute-start.2 = (bf16[3,1,64,32]{2,3,1,0:T(8,128)(2,1)S(1)}, bf16[3,1,64,32]{2,3,1,0:T(8,128)(2,1)S(1)}, u32[]{:S(2)}, u32[]{:S(2)}) collective-permute-start(bf16[3,1,64,32]{2,3,1,0:T(8,128)(2,1)S(1)} %get-tuple-element.68), channel_id=1, source_target_pairs={{0,1},{1,2},{2,3},{3,4},{4,5},{5,6},{6,7},{8,9},{9,10},{10,11},{11... | collective-permute-start | bytes 36872 | tf_op jit(solution)/shard_map/ppermute | solution.py:15
  24.1 26.2 %all_gather.3 = bf16[1,8,64,256]{2,1,0,3:T(8,128)(2,1)S(1)} all-gather(bf16[1,8,64,32]{2,1,0,3:T(8,128)(2,1)S(1)} %copy.98), channel_id=1, replica_groups=mesh['chan'=8,'sx'=8,'sy'=8] {'chan'}, dimensions={3}, use_global_device_ids=true | all-gather | bytes 294912 | tf_op jit(solution)/shard_map/all_gather | solution.py:39
  50.6 5.5 %collective-permute-start.5 = (bf16[1,8,64,256]{3,2,1,0:T(8,128)(2,1)S(1)}, bf16[1,8,64,256]{3,2,1,0:T(8,128)(2,1)S(1)}, u32[]{:S(2)}, u32[]{:S(2)}) collective-permute-start(bf16[1,8,64,256]{3,2,1,0:T(8,128)(2,1)S(1)} %copy.99), channel_id=1, source_target_pairs={{8,0},{16,8},{24,16},{32,24},{40,32},{48,40},{56,48},{9,1},{17,9},... | collective-permute-start | bytes 786440 | tf_op jit(solution)/shard_map/ppermute | solution.py:16
  56.1 4.7 %collective-permute-start.4 = (bf16[1,8,64,256]{3,2,1,0:T(8,128)(2,1)S(1)}, bf16[1,8,64,256]{3,2,1,0:T(8,128)(2,1)S(1)}, u32[]{:S(2)}, u32[]{:S(2)}) collective-permute-start(bf16[1,8,64,256]{3,2,1,0:T(8,128)(2,1)S(1)} %copy.99), channel_id=1, source_target_pairs={{0,8},{8,16},{16,24},{24,32},{32,40},{40,48},{48,56},{1,9},{9,17},... | collective-permute-start | bytes 786440 | tf_op jit(solution)/shard_map/ppermute | solution.py:15
  74.5 1.6 reshape.329
  77.6 1.6 reshape.330
  83.7 1.6 reshape.332
  88.1 1.6 reshape.334
  90.3 1.6 reshape.335
  93.4 1.6 reshape.337
  96.4 1.6 reshape.338
  100.9 1.6 reshape.340
  103.9 1.6 reshape.341
  109.2 1.6 reshape.343
  112.2 1.6 reshape.344
  114.5 1.6 reshape.347
  146.8 1.9 collective-permute-start.7
  148.7 4.8 %collective-permute-start.6 = (bf16[3,1,64,256]{3,2,1,0:T(8,128)(2,1)S(1)}, bf16[3,1,64,256]{3,2,1,0:T(8,128)(2,1)S(1)}, u32[]{:S(2)}, u32[]{:S(2)}) collective-permute-start(bf16[3,1,64,256]{3,2,1,0:T(8,128)(2,1)S(1)} %get-tuple-element.39), channel_id=1, source_target_pairs={{0,1},{1,2},{2,3},{3,4},{4,5},{5,6},{6,7},{8,9},{9,10},{10,11},{11... | collective-permute-start | bytes 294920 | tf_op jit(solution)/shard_map/ppermute | solution.py:15
  162.8 168.9 %all-reduce.4.cloned.1.call-done = f32[27,32,256]{2,1,0:T(8,128)} async-done(((f32[27,32,256]{2,1,0:T(8,128)}), f32[27,32,256]{2,1,0:T(8,128)}) %all-reduce.4.cloned.1.call-update) | async-done | bytes 884752 | tf_op jit(solution)/shard_map/psum | solution.py:61
  331.7 2.2 broadcast_multiply_fusion
  (229 shorter events, 79.6 us)
Async XLA Ops:
  8.0 52.8 %copy-start.4 = (bf16[1,8,64,32]{2,3,1,0:T(8,128)(2,1)S(1)}, bf16[1,8,64,32]{2,3,1,0:T(8,128)(2,1)}, u32[]{:S(2)}) copy-start(bf16[1,8,64,32]{2,3,1,0:T(8,128)(2,1)} %param.3) | copy-start | bytes 98308
  8.0 323.7 %all-reduce.4.cloned.1.call-start = ((), (), s32[]{:S(2)}) async-start(), calls=%async_computation.2 | async-start | bytes 1769472 | tf_op jit(solution)/shard_map/psum | solution.py:61
  8.1 6.5 %collective-permute-start = (bf16[1,8,64,32]{2,3,1,0:T(8,128)(2,1)}, bf16[1,8,64,32]{2,3,1,0:T(8,128)(2,1)S(1)}, u32[]{:S(2)}, u32[]{:S(2)}) collective-permute-start(bf16[1,8,64,32]{2,3,1,0:T(8,128)(2,1)} %param.3), channel_id=1, source_target_pairs={{0,8},{8,16},{16,24},{24,32},{32,40},{40,48},{48,56},{1,9},{9,17},... | collective-permute-start | bytes 98312 | tf_op jit(solution)/shard_map/ppermute | solution.py:15
  11.7 5.8 %collective-permute-start.1 = (bf16[1,8,64,32]{2,3,1,0:T(8,128)(2,1)}, bf16[1,8,64,32]{2,3,1,0:T(8,128)(2,1)S(1)}, u32[]{:S(2)}, u32[]{:S(2)}) collective-permute-start(bf16[1,8,64,32]{2,3,1,0:T(8,128)(2,1)} %param.3), channel_id=1, source_target_pairs={{8,0},{16,8},{24,16},{32,24},{40,32},{48,40},{56,48},{9,1},{17,9},... | collective-permute-start | bytes 98312 | tf_op jit(solution)/shard_map/ppermute | solution.py:16
  14.6 47.1 %copy-start.8 = (bf16[1,8,64,32]{2,3,1,0:T(8,128)(2,1)}, bf16[1,8,64,32]{2,3,1,0:T(8,128)(2,1)S(1)}, u32[]{:S(2)}) copy-start(bf16[1,8,64,32]{2,3,1,0:T(8,128)(2,1)S(1)} %collective-permute-done) | copy-start | bytes 98308
  17.5 45.0 %copy-start.6 = (bf16[1,8,64,32]{2,3,1,0:T(8,128)(2,1)}, bf16[1,8,64,32]{2,3,1,0:T(8,128)(2,1)S(1)}, u32[]{:S(2)}) copy-start(bf16[1,8,64,32]{2,3,1,0:T(8,128)(2,1)S(1)} %collective-permute-done.1) | copy-start | bytes 98308
  17.6 44.9 %collective-permute-start.3 = (bf16[3,1,64,32]{2,3,1,0:T(8,128)(2,1)S(1)}, bf16[3,1,64,32]{2,3,1,0:T(8,128)(2,1)S(1)}, u32[]{:S(2)}, u32[]{:S(2)}) collective-permute-start(bf16[3,1,64,32]{2,3,1,0:T(8,128)(2,1)S(1)} %get-tuple-element.69), channel_id=1, source_target_pairs={{1,0},{2,1},{3,2},{4,3},{5,4},{6,5},{7,6},{9,8},{10,9},{11,10},{12... | collective-permute-start | bytes 36872 | tf_op jit(solution)/shard_map/ppermute | solution.py:16
  19.7 42.9 %collective-permute-start.2 = (bf16[3,1,64,32]{2,3,1,0:T(8,128)(2,1)S(1)}, bf16[3,1,64,32]{2,3,1,0:T(8,128)(2,1)S(1)}, u32[]{:S(2)}, u32[]{:S(2)}) collective-permute-start(bf16[3,1,64,32]{2,3,1,0:T(8,128)(2,1)S(1)} %get-tuple-element.68), channel_id=1, source_target_pairs={{0,1},{1,2},{2,3},{3,4},{4,5},{5,6},{6,7},{8,9},{9,10},{10,11},{11... | collective-permute-start | bytes 36872 | tf_op jit(solution)/shard_map/ppermute | solution.py:15
  50.6 96.1 %collective-permute-start.5 = (bf16[1,8,64,256]{3,2,1,0:T(8,128)(2,1)S(1)}, bf16[1,8,64,256]{3,2,1,0:T(8,128)(2,1)S(1)}, u32[]{:S(2)}, u32[]{:S(2)}) collective-permute-start(bf16[1,8,64,256]{3,2,1,0:T(8,128)(2,1)S(1)} %copy.99), channel_id=1, source_target_pairs={{8,0},{16,8},{24,16},{32,24},{40,32},{48,40},{56,48},{9,1},{17,9},... | collective-permute-start | bytes 786440 | tf_op jit(solution)/shard_map/ppermute | solution.py:16
  56.1 90.7 %collective-permute-start.4 = (bf16[1,8,64,256]{3,2,1,0:T(8,128)(2,1)S(1)}, bf16[1,8,64,256]{3,2,1,0:T(8,128)(2,1)S(1)}, u32[]{:S(2)}, u32[]{:S(2)}) collective-permute-start(bf16[1,8,64,256]{3,2,1,0:T(8,128)(2,1)S(1)} %copy.99), channel_id=1, source_target_pairs={{0,8},{8,16},{16,24},{24,32},{32,40},{40,48},{48,56},{1,9},{9,17},... | collective-permute-start | bytes 786440 | tf_op jit(solution)/shard_map/ppermute | solution.py:15
  63.9 2.3 copy-start
  68.5 18.9 %copy-start.14 = (bf16[1,8,64,32]{2,3,1,0:T(8,128)(2,1)S(1)}, bf16[1,8,64,32]{2,3,1,0:T(8,128)(2,1)}, u32[]{:S(2)}) copy-start(bf16[1,8,64,32]{2,3,1,0:T(8,128)(2,1)} %get-tuple-element.51) | copy-start | bytes 98308
  68.5 21.2 %copy-start.13 = (bf16[1,8,64,32]{2,3,1,0:T(8,128)(2,1)S(1)}, bf16[1,8,64,32]{2,3,1,0:T(8,128)(2,1)}, u32[]{:S(2)}) copy-start(bf16[1,8,64,32]{2,3,1,0:T(8,128)(2,1)} %get-tuple-element.50) | copy-start | bytes 98308
  74.5 25.7 %copy-start.12 = (bf16[1,8,64,32]{2,3,1,0:T(8,128)(2,1)S(1)}, bf16[1,8,64,32]{2,3,1,0:T(8,128)(2,1)}, u32[]{:S(2)}) copy-start(bf16[1,8,64,32]{2,3,1,0:T(8,128)(2,1)} %get-tuple-element.47) | copy-start | bytes 98308
  88.1 25.7 %copy-start.11 = (bf16[1,8,64,32]{2,3,1,0:T(8,128)(2,1)S(1)}, bf16[1,8,64,32]{2,3,1,0:T(8,128)(2,1)}, u32[]{:S(2)}) copy-start(bf16[1,8,64,32]{2,3,1,0:T(8,128)(2,1)} %get-tuple-element.42) | copy-start | bytes 98308
  90.3 25.7 %copy-start.3 = (bf16[1,8,64,32]{2,3,1,0:T(8,128)(2,1)S(1)}, bf16[1,8,64,32]{2,3,1,0:T(8,128)(2,1)}, u32[]{:S(2)}) copy-start(bf16[1,8,64,32]{2,3,1,0:T(8,128)(2,1)} %copy-done.2) | copy-start | bytes 98308
  102.4 16.1 %copy-start.9 = (bf16[1,8,64,32]{2,3,1,0:T(8,128)(2,1)S(1)}, bf16[1,8,64,32]{2,3,1,0:T(8,128)(2,1)}, u32[]{:S(2)}) copy-start(bf16[1,8,64,32]{2,3,1,0:T(8,128)(2,1)} %copy-done.8) | copy-start | bytes 98308
  116.0 5.0 %copy-start.1 = (bf16[1,8,64,32]{2,3,1,0:T(8,128)(2,1)S(1)}, bf16[1,8,64,32]{2,3,1,0:T(8,128)(2,1)}, u32[]{:S(2)}) copy-start(bf16[1,8,64,32]{2,3,1,0:T(8,128)(2,1)} %get-tuple-element.60) | copy-start | bytes 98308
  121.0 5.0 %copy-start.5 = (bf16[1,8,64,32]{2,3,1,0:T(8,128)(2,1)S(1)}, bf16[1,8,64,32]{2,3,1,0:T(8,128)(2,1)}, u32[]{:S(2)}) copy-start(bf16[1,8,64,32]{2,3,1,0:T(8,128)(2,1)} %param.3) | copy-start | bytes 98308
  128.6 5.0 %copy-start.7 = (bf16[1,8,64,32]{2,3,1,0:T(8,128)(2,1)S(1)}, bf16[1,8,64,32]{2,3,1,0:T(8,128)(2,1)}, u32[]{:S(2)}) copy-start(bf16[1,8,64,32]{2,3,1,0:T(8,128)(2,1)} %copy-done.6) | copy-start | bytes 98308
  134.4 3.5 %copy-start.17 = (bf16[512,32]{0,1:T(8,128)(2,1)S(1)}, bf16[512,32]{0,1:T(8,128)(2,1)}, u32[]{:S(2)}) copy-start(bf16[512,32]{0,1:T(8,128)(2,1)} %reshape.324) | copy-start | bytes 98308
  137.8 196.1 %reduce-scatter.2.cloned.1.call-start = ((), (), s32[]{:S(2)}) async-start(), calls=%async_computation.1 | async-start | bytes 1179648 | tf_op jit(solution)/shard_map/reduce_scatter | solution.py:36
  146.8 8.3 %collective-permute-start.7 = (bf16[3,1,64,256]{3,2,1,0:T(8,128)(2,1)S(1)}, bf16[3,1,64,256]{3,2,1,0:T(8,128)(2,1)S(1)}, u32[]{:S(2)}, u32[]{:S(2)}) collective-permute-start(bf16[3,1,64,256]{3,2,1,0:T(8,128)(2,1)S(1)} %get-tuple-element.40), channel_id=1, source_target_pairs={{1,0},{2,1},{3,2},{4,3},{5,4},{6,5},{7,6},{9,8},{10,9},{11,10},{12... | collective-permute-start | bytes 294920 | tf_op jit(solution)/shard_map/ppermute | solution.py:16
  148.7 6.4 %collective-permute-start.6 = (bf16[3,1,64,256]{3,2,1,0:T(8,128)(2,1)S(1)}, bf16[3,1,64,256]{3,2,1,0:T(8,128)(2,1)S(1)}, u32[]{:S(2)}, u32[]{:S(2)}) collective-permute-start(bf16[3,1,64,256]{3,2,1,0:T(8,128)(2,1)S(1)} %get-tuple-element.39), channel_id=1, source_target_pairs={{0,1},{1,2},{2,3},{3,4},{4,5},{5,6},{6,7},{8,9},{9,10},{10,11},{11... | collective-permute-start | bytes 294920 | tf_op jit(solution)/shard_map/ppermute | solution.py:15
  (24 other events, 18.4 us)
Sparse Core Ops, SparseCore 0:
  137.9 193.7 all-reduce.3
Sparse Core Ops, SparseCore 1:
  155.2 32.7 reduce-scatter.1
where the time goes:
time: 345 us; the launch traced here: 343 us
  waiting for transfers between devices  171 us (50%)
  local copies, waits for them, and re-layouts  60 us (17%)
  matrix products  34.2 us (10%)
  starting transfers between devices  29 us (8%)
  blocking collectives  26.2 us (8%)
  between operations  16.2 us (5%)
  other arithmetic  6.23 us (2%)
    psum x1, waiting for transfers between devices, body(): summed = lax.psum(local_kernel, ('sx', 'sy'))  169 us
    reshape x27, local copies, waits for them, and re-layouts, body(): padded[a:a + size_x, b:b + size_y, e:e + size_z].reshape(cells, own_in)  29.3 us
    all_gather x1, blocking collectives, body(): grad_full = lax.all_gather(grad_out, 'chan', axis=3, tiled=True)  26.2 us
    dot_general x27, matrix products, body(): lax.dot_general(in_window, flat_grad, (((0,), (0,)), ((), ())), preferred...  22.6 us
    slice x25, local copies, waits for them, and re-layouts, body(): padded[a:a + size_x, b:b + size_y, e:e + size_z].reshape(cells, own_in)  21 us
    ppermute x4, starting transfers between devices, padded_2(): before = lax.ppermute(last, axis, up)  17.6 us
    ppermute x4, starting transfers between devices, padded_2(): after = lax.ppermute(leading, axis, down)  11.4 us
    unnamed x81, local copies, waits for them, and re-layouts  6.98 us
  transfers between devices with their start and end apart: 10, of which 2 were waited for; matrix products, arithmetic and copies ran while one was open for 28% of the time, Pallas kernels for 0%

commit v1 on v0

--- a/solution.py
+++ b/solution.py
@@ -58,7 +58,8 @@
         )
     grad_input = back.reshape(size_x, size_y, size_z, own_in).astype(jnp.bfloat16)
     local_kernel = jnp.stack(kernel_terms)
-    summed = lax.psum(local_kernel, ("sx", "sy"))
+    half = lax.psum(local_kernel, "sx")
+    summed = lax.psum(half, "sy")
     all_cells = cells * lax.axis_size("sx") * lax.axis_size("sy")
     grad_kernel = summed / jnp.float32(math.sqrt(all_cells))
     return (out, grad_input, grad_kernel)

time: 345 us -> 301 us (0.87)
  the two profiles are of different devices: /device:TPU:25 before, /device:TPU:2 now
where the time goes in v1:
time: 301 us; the launch traced here: 299 us
  waiting for transfers between devices  128 us (43%)
  local copies, waits for them, and re-layouts  60 us (20%)
  matrix products  34.2 us (11%)
  blocking collectives  31.9 us (11%)
  starting transfers between devices  21.9 us (7%)
  between operations  16.2 us (5%)
  other arithmetic  6.23 us (2%)
    psum x1, waiting for transfers between devices, body(): summed = lax.psum(half, 'sy')  80.5 us
    psum x1, waiting for transfers between devices, body(): half = lax.psum(local_kernel, 'sx')  46.2 us
    all_gather x1, blocking collectives, body(): grad_full = lax.all_gather(grad_out, 'chan', axis=3, tiled=True)  31.9 us
    reshape x27, local copies, waits for them, and re-layouts, body(): padded[a:a + size_x, b:b + size_y, e:e + size_z].reshape(cells, own_in)  29.3 us
    dot_general x27, matrix products, body(): lax.dot_general(in_window, flat_grad, (((0,), (0,)), ((), ())), preferred...  22.6 us
    slice x25, local copies, waits for them, and re-layouts, body(): padded[a:a + size_x, b:b + size_y, e:e + size_z].reshape(cells, own_in)  21 us
    ppermute x4, starting transfers between devices, padded_2(): before = lax.ppermute(last, axis, up)  13.4 us
    ppermute x4, starting transfers between devices, padded_2(): after = lax.ppermute(leading, axis, down)  8.15 us
  transfers between devices with their start and end apart: 11, of which 4 were waited for; matrix products, arithmetic and copies ran while one was open for 31% of the time, Pallas kernels for 0%

profile of v1, /device:TPU:2, one launch (start us, length us, event | category | flops | bytes accessed | tf_op | source)
XLA Modules:
  0.0 298.6 jit_solution(353161045384151062)
XLA Ops:
  8.1 1.9 collective-permute-start
  10.0 3.6 %collective-permute-start.1 = (bf16[1,8,64,32]{2,3,1,0:T(8,128)(2,1)}, bf16[1,8,64,32]{2,3,1,0:T(8,128)(2,1)S(1)}, u32[]{:S(2)}, u32[]{:S(2)}) collective-permute-start(bf16[1,8,64,32]{2,3,1,0:T(8,128)(2,1)} %param.3), channel_id=1, source_target_pairs={{8,0},{16,8},{24,16},{32,24},{40,32},{48,40},{56,48},{9,1},{17,9},... | collective-permute-start | bytes 98312 | tf_op jit(solution)/shard_map/ppermute | solution.py:16
  17.2 4.5 %collective-permute-start.2 = (bf16[3,1,64,32]{2,3,1,0:T(8,128)(2,1)S(1)}, bf16[3,1,64,32]{2,3,1,0:T(8,128)(2,1)S(1)}, u32[]{:S(2)}, u32[]{:S(2)}) collective-permute-start(bf16[3,1,64,32]{2,3,1,0:T(8,128)(2,1)S(1)} %get-tuple-element.68), channel_id=1, source_target_pairs={{0,1},{1,2},{2,3},{3,4},{4,5},{5,6},{6,7},{8,9},{9,10},{10,11},{11... | collective-permute-start | bytes 36872 | tf_op jit(solution)/shard_map/ppermute | solution.py:15
  21.7 31.9 %all_gather.3 = bf16[1,8,64,256]{2,1,0,3:T(8,128)(2,1)S(1)} all-gather(bf16[1,8,64,32]{2,1,0,3:T(8,128)(2,1)S(1)} %copy.98), channel_id=1, replica_groups=mesh['chan'=8,'sx'=8,'sy'=8] {'chan'}, dimensions={3}, use_global_device_ids=true | all-gather | bytes 294912 | tf_op jit(solution)/shard_map/all_gather | solution.py:39
  54.0 1.9 collective-permute-start.5
  55.9 2.4 collective-permute-start.4
  72.0 1.6 reshape.329
  75.1 1.6 reshape.330
  78.2 1.6 reshape.331
  81.2 1.6 reshape.332
  85.6 1.6 reshape.334
  87.8 1.6 reshape.335
  90.9 1.6 reshape.337
  94.0 1.6 reshape.338
  98.4 1.6 reshape.340
  101.4 1.6 reshape.341
  103.6 1.6 reshape.342
  106.7 1.6 reshape.343
  109.7 1.6 reshape.344
  112.0 1.6 reshape.347
  145.6 4.6 %collective-permute-start.6 = (bf16[3,1,64,256]{3,2,1,0:T(8,128)(2,1)S(1)}, bf16[3,1,64,256]{3,2,1,0:T(8,128)(2,1)S(1)}, u32[]{:S(2)}, u32[]{:S(2)}) collective-permute-start(bf16[3,1,64,256]{3,2,1,0:T(8,128)(2,1)S(1)} %get-tuple-element.39), channel_id=1, source_target_pairs={{0,1},{1,2},{2,3},{3,4},{4,5},{5,6},{6,7},{8,9},{9,10},{10,11},{11... | collective-permute-start | bytes 294920 | tf_op jit(solution)/shard_map/ppermute | solution.py:15
  159.1 46.2 %all-reduce.5.cloned.1.call-done = f32[27,32,256]{2,1,0:T(8,128)} async-done(((f32[27,32,256]{2,1,0:T(8,128)}), f32[27,32,256]{2,1,0:T(8,128)}) %all-reduce.5.cloned.1.call-update) | async-done | bytes 884752 | tf_op jit(solution)/shard_map/psum | solution.py:61
  208.4 80.5 %all-reduce.7.cloned.1.call-done = f32[27,32,256]{2,1,0:T(8,128)} async-done(((f32[27,32,256]{2,1,0:T(8,128)}), f32[27,32,256]{2,1,0:T(8,128)}) %all-reduce.7.cloned.1.call-update) | async-done | bytes 884752 | tf_op jit(solution)/shard_map/psum | solution.py:62
  288.9 2.2 broadcast_multiply_fusion
  (232 shorter events, 80.7 us)
Async XLA Ops:
  8.0 50.3 %copy-start.4 = (bf16[1,8,64,32]{2,3,1,0:T(8,128)(2,1)S(1)}, bf16[1,8,64,32]{2,3,1,0:T(8,128)(2,1)}, u32[]{:S(2)}) copy-start(bf16[1,8,64,32]{2,3,1,0:T(8,128)(2,1)} %param.3) | copy-start | bytes 98308
  8.0 197.3 %all-reduce.5.cloned.1.call-start = ((), (), s32[]{:S(2)}) async-start(), calls=%async_computation.2 | async-start | bytes 1769472 | tf_op jit(solution)/shard_map/psum | solution.py:61
  8.1 6.5 %collective-permute-start = (bf16[1,8,64,32]{2,3,1,0:T(8,128)(2,1)}, bf16[1,8,64,32]{2,3,1,0:T(8,128)(2,1)S(1)}, u32[]{:S(2)}, u32[]{:S(2)}) collective-permute-start(bf16[1,8,64,32]{2,3,1,0:T(8,128)(2,1)} %param.3), channel_id=1, source_target_pairs={{0,8},{8,16},{16,24},{24,32},{32,40},{40,48},{48,56},{1,9},{9,17},... | collective-permute-start | bytes 98312 | tf_op jit(solution)/shard_map/ppermute | solution.py:15
  10.0 5.9 %collective-permute-start.1 = (bf16[1,8,64,32]{2,3,1,0:T(8,128)(2,1)}, bf16[1,8,64,32]{2,3,1,0:T(8,128)(2,1)S(1)}, u32[]{:S(2)}, u32[]{:S(2)}) collective-permute-start(bf16[1,8,64,32]{2,3,1,0:T(8,128)(2,1)} %param.3), channel_id=1, source_target_pairs={{8,0},{16,8},{24,16},{32,24},{40,32},{48,40},{56,48},{9,1},{17,9},... | collective-permute-start | bytes 98312 | tf_op jit(solution)/shard_map/ppermute | solution.py:16
  14.5 44.6 %copy-start.8 = (bf16[1,8,64,32]{2,3,1,0:T(8,128)(2,1)}, bf16[1,8,64,32]{2,3,1,0:T(8,128)(2,1)S(1)}, u32[]{:S(2)}) copy-start(bf16[1,8,64,32]{2,3,1,0:T(8,128)(2,1)S(1)} %collective-permute-done) | copy-start | bytes 98308
  15.8 44.2 %copy-start.6 = (bf16[1,8,64,32]{2,3,1,0:T(8,128)(2,1)}, bf16[1,8,64,32]{2,3,1,0:T(8,128)(2,1)S(1)}, u32[]{:S(2)}) copy-start(bf16[1,8,64,32]{2,3,1,0:T(8,128)(2,1)S(1)} %collective-permute-done.1) | copy-start | bytes 98308
  15.9 44.2 %collective-permute-start.3 = (bf16[3,1,64,32]{2,3,1,0:T(8,128)(2,1)S(1)}, bf16[3,1,64,32]{2,3,1,0:T(8,128)(2,1)S(1)}, u32[]{:S(2)}, u32[]{:S(2)}) collective-permute-start(bf16[3,1,64,32]{2,3,1,0:T(8,128)(2,1)S(1)} %get-tuple-element.69), channel_id=1, source_target_pairs={{1,0},{2,1},{3,2},{4,3},{5,4},{6,5},{7,6},{9,8},{10,9},{11,10},{12... | collective-permute-start | bytes 36872 | tf_op jit(solution)/shard_map/ppermute | solution.py:16
  17.2 42.9 %collective-permute-start.2 = (bf16[3,1,64,32]{2,3,1,0:T(8,128)(2,1)S(1)}, bf16[3,1,64,32]{2,3,1,0:T(8,128)(2,1)S(1)}, u32[]{:S(2)}, u32[]{:S(2)}) collective-permute-start(bf16[3,1,64,32]{2,3,1,0:T(8,128)(2,1)S(1)} %get-tuple-element.68), channel_id=1, source_target_pairs={{0,1},{1,2},{2,3},{3,4},{4,5},{5,6},{6,7},{8,9},{9,10},{10,11},{11... | collective-permute-start | bytes 36872 | tf_op jit(solution)/shard_map/ppermute | solution.py:15
  54.0 90.3 %collective-permute-start.5 = (bf16[1,8,64,256]{3,2,1,0:T(8,128)(2,1)S(1)}, bf16[1,8,64,256]{3,2,1,0:T(8,128)(2,1)S(1)}, u32[]{:S(2)}, u32[]{:S(2)}) collective-permute-start(bf16[1,8,64,256]{3,2,1,0:T(8,128)(2,1)S(1)} %copy.99), channel_id=1, source_target_pairs={{8,0},{16,8},{24,16},{32,24},{40,32},{48,40},{56,48},{9,1},{17,9},... | collective-permute-start | bytes 786440 | tf_op jit(solution)/shard_map/ppermute | solution.py:16
  55.9 88.4 %collective-permute-start.4 = (bf16[1,8,64,256]{3,2,1,0:T(8,128)(2,1)S(1)}, bf16[1,8,64,256]{3,2,1,0:T(8,128)(2,1)S(1)}, u32[]{:S(2)}, u32[]{:S(2)}) collective-permute-start(bf16[1,8,64,256]{3,2,1,0:T(8,128)(2,1)S(1)} %copy.99), channel_id=1, source_target_pairs={{0,8},{8,16},{16,24},{24,32},{32,40},{40,48},{48,56},{1,9},{9,17},... | collective-permute-start | bytes 786440 | tf_op jit(solution)/shard_map/ppermute | solution.py:15
  66.0 18.9 %copy-start.14 = (bf16[1,8,64,32]{2,3,1,0:T(8,128)(2,1)S(1)}, bf16[1,8,64,32]{2,3,1,0:T(8,128)(2,1)}, u32[]{:S(2)}) copy-start(bf16[1,8,64,32]{2,3,1,0:T(8,128)(2,1)} %get-tuple-element.51) | copy-start | bytes 98308
  66.0 21.2 %copy-start.13 = (bf16[1,8,64,32]{2,3,1,0:T(8,128)(2,1)S(1)}, bf16[1,8,64,32]{2,3,1,0:T(8,128)(2,1)}, u32[]{:S(2)}) copy-start(bf16[1,8,64,32]{2,3,1,0:T(8,128)(2,1)} %get-tuple-element.50) | copy-start | bytes 98308
  72.0 25.7 %copy-start.12 = (bf16[1,8,64,32]{2,3,1,0:T(8,128)(2,1)S(1)}, bf16[1,8,64,32]{2,3,1,0:T(8,128)(2,1)}, u32[]{:S(2)}) copy-start(bf16[1,8,64,32]{2,3,1,0:T(8,128)(2,1)} %get-tuple-element.47) | copy-start | bytes 98308
  85.6 25.7 %copy-start.11 = (bf16[1,8,64,32]{2,3,1,0:T(8,128)(2,1)S(1)}, bf16[1,8,64,32]{2,3,1,0:T(8,128)(2,1)}, u32[]{:S(2)}) copy-start(bf16[1,8,64,32]{2,3,1,0:T(8,128)(2,1)} %get-tuple-element.42) | copy-start | bytes 98308
  87.8 25.7 %copy-start.3 = (bf16[1,8,64,32]{2,3,1,0:T(8,128)(2,1)S(1)}, bf16[1,8,64,32]{2,3,1,0:T(8,128)(2,1)}, u32[]{:S(2)}) copy-start(bf16[1,8,64,32]{2,3,1,0:T(8,128)(2,1)} %copy-done.2) | copy-start | bytes 98308
  99.9 16.1 %copy-start.9 = (bf16[1,8,64,32]{2,3,1,0:T(8,128)(2,1)S(1)}, bf16[1,8,64,32]{2,3,1,0:T(8,128)(2,1)}, u32[]{:S(2)}) copy-start(bf16[1,8,64,32]{2,3,1,0:T(8,128)(2,1)} %copy-done.8) | copy-start | bytes 98308
  113.5 5.0 %copy-start.1 = (bf16[1,8,64,32]{2,3,1,0:T(8,128)(2,1)S(1)}, bf16[1,8,64,32]{2,3,1,0:T(8,128)(2,1)}, u32[]{:S(2)}) copy-start(bf16[1,8,64,32]{2,3,1,0:T(8,128)(2,1)} %get-tuple-element.60) | copy-start | bytes 98308
  118.6 5.0 %copy-start.5 = (bf16[1,8,64,32]{2,3,1,0:T(8,128)(2,1)S(1)}, bf16[1,8,64,32]{2,3,1,0:T(8,128)(2,1)}, u32[]{:S(2)}) copy-start(bf16[1,8,64,32]{2,3,1,0:T(8,128)(2,1)} %param.3) | copy-start | bytes 98308
  126.1 5.0 %copy-start.7 = (bf16[1,8,64,32]{2,3,1,0:T(8,128)(2,1)S(1)}, bf16[1,8,64,32]{2,3,1,0:T(8,128)(2,1)}, u32[]{:S(2)}) copy-start(bf16[1,8,64,32]{2,3,1,0:T(8,128)(2,1)} %copy-done.6) | copy-start | bytes 98308
  131.9 3.5 %copy-start.17 = (bf16[512,32]{0,1:T(8,128)(2,1)S(1)}, bf16[512,32]{0,1:T(8,128)(2,1)}, u32[]{:S(2)}) copy-start(bf16[512,32]{0,1:T(8,128)(2,1)} %reshape.324) | copy-start | bytes 98308
  135.3 71.5 %reduce-scatter.2.cloned.1.call-start = ((), (), s32[]{:S(2)}) async-start(), calls=%async_computation.1 | async-start | bytes 1179648 | tf_op jit(solution)/shard_map/reduce_scatter | solution.py:36
  144.3 7.7 %collective-permute-start.7 = (bf16[3,1,64,256]{3,2,1,0:T(8,128)(2,1)S(1)}, bf16[3,1,64,256]{3,2,1,0:T(8,128)(2,1)S(1)}, u32[]{:S(2)}, u32[]{:S(2)}) collective-permute-start(bf16[3,1,64,256]{3,2,1,0:T(8,128)(2,1)S(1)} %get-tuple-element.40), channel_id=1, source_target_pairs={{1,0},{2,1},{3,2},{4,3},{5,4},{6,5},{7,6},{9,8},{10,9},{11,10},{12... | collective-permute-start | bytes 294920 | tf_op jit(solution)/shard_map/ppermute | solution.py:16
  145.6 7.4 %collective-permute-start.6 = (bf16[3,1,64,256]{3,2,1,0:T(8,128)(2,1)S(1)}, bf16[3,1,64,256]{3,2,1,0:T(8,128)(2,1)S(1)}, u32[]{:S(2)}, u32[]{:S(2)}) collective-permute-start(bf16[3,1,64,256]{3,2,1,0:T(8,128)(2,1)S(1)} %get-tuple-element.39), channel_id=1, source_target_pairs={{0,1},{1,2},{2,3},{3,4},{4,5},{5,6},{6,7},{8,9},{9,10},{10,11},{11... | collective-permute-start | bytes 294920 | tf_op jit(solution)/shard_map/ppermute | solution.py:15
  151.8 137.1 %all-reduce.7.cloned.1.call-start = ((), (), s32[]{:S(2)}) async-start(), calls=%async_computation.3 | async-start | bytes 1769472 | tf_op jit(solution)/shard_map/psum | solution.py:62
  (25 other events, 20.6 us)
Sparse Core Ops, SparseCore 0:
  135.5 69.7 all-reduce.4
  207.8 81.0 all-reduce.6
Sparse Core Ops, SparseCore 1:
  151.9 40.4 reduce-scatter.1
